TPU v7x, 32 devices: a whole 2x2x4 slice. The times are simulated.
32 devices in a mesh: gx: 2 (over y), gy: 4 (over z), gz: 4 (over x, core).
Axes of the slice: x: 2, y: 2, z: 4, core: 2. Of those that a mesh axis runs over, the one named last changes fastest.
Arguments:
- features: bfloat16 [64, 2, 4, 8192], P(None, 'gx', 'gy', 'gz'), may hold values from -6 to 6
- tiles: bfloat16 [2, 4, 128, 64, 512], P('gx', 'gy', 'gz'), may hold values from -0.25 to 0.25
- scales: float32 [2, 4, 128, 8], P('gx', 'gy', 'gz'), may hold values from 0.5 to 2
- slots: int32 [2, 4, 128, 8], P('gx', 'gy', 'gz'), may hold values from 0 to 175, as said below
- live: int32 [2, 4, 128], P('gx', 'gy', 'gz'), may hold values from 2 to 8, as said below
- times: float32 [64], replicated, may hold values from 0.6 to 1.6
Outputs:
- diffused: bfloat16 [64, 2, 4, 8192], P(None, 'gx', 'gy', 'gz')
Inputs may be any that keep to these rules, and one draw needn't show every extreme that they name: Slot 0 of every block row is the row's own block; slots 1 to 3 hold blocks of the row's own device, the others blocks from the shared set. `live`: each device has some block row with all 8 slots used.
All inputs are finite; a program needn't handle non-finite values.
Results may differ from a plain program's by a relative error of at most 0.0032.
Values may be sent and summed in bfloat16 or wider, within the bound.
No kernel may reach another device: no remote copies, remote signals or barrier semaphores. Data moves between devices by JAX's collectives and lax.ppermute only.
A program may use at most 64 MiB of HBM per device.

v0:
```python
import jax
import jax.numpy as jnp
from jax import lax
from jax.sharding import PartitionSpec as P

PB = 64
TERMS = 3


def with_halo(cells, sides, width):
    for axis, dim in sides:
        count = lax.axis_size(axis)
        ends = count - 1
        head = lax.slice_in_dim(cells, 0, width, axis=dim)
        tail = lax.slice_in_dim(cells, cells.shape[dim] - width, cells.shape[dim], axis=dim)
        cells = jnp.concatenate(
            [
                lax.ppermute(tail, axis, [(i, (i + 1) % count) for i in range(ends)]),
                cells,
                lax.ppermute(head, axis, [((i + 1) % count, i) for i in range(ends)]),
            ],
            axis=dim,
        )
    return cells


def to_blocks(value):
    count = value.shape[3] // PB
    return (
        value.reshape(value.shape[0], count, PB)
        .transpose(1, 0, 2)
        .reshape(count, value.shape[0] * PB)
    )


def shared_blocks(rim_rows):
    width = rim_rows.shape[1]
    panel = lax.all_gather(rim_rows, "gz", axis=0, tiled=True)
    grid = with_halo(panel.reshape(1, 1, panel.shape[0], width), (("gx", 0), ("gy", 1)), 1)
    return grid.reshape(-1, width)


def apply_operator(value, tile_rows, scale_rows, slot_rows, live_rows):
    blocks = to_blocks(value)
    count = blocks.shape[0]
    slot_count = slot_rows.shape[1]
    rim_count = max(1, count // 8)
    source = jnp.concatenate([blocks, shared_blocks(blocks[:rim_count])], 0)
    picked = jnp.take(source, slot_rows.reshape(-1), axis=0).reshape(
        count, slot_count, value.shape[0], PB
    )
    tile_parts = tile_rows.reshape(count, PB, slot_count, PB)
    used = (lax.broadcasted_iota(jnp.int32, (count, slot_count), 1) < live_rows[:, None]).astype(
        jnp.float32
    )
    weights = scale_rows * used
    result = jnp.zeros((count, value.shape[0], PB), jnp.float32)
    for slot in range(slot_count):
        partial_rows = jnp.einsum(
            "bfc,brc->bfr",
            picked[:, slot],
            tile_parts[:, :, slot],
            preferred_element_type=jnp.float32,
        )
        result = result + weights[:, slot][:, None, None] * partial_rows
    return result.transpose(1, 0, 2).reshape(value.shape[0], 1, 1, count * PB)


def body(features, tiles, scales, slots, live, times):
    count = tiles.shape[2]
    tile_rows = tiles.reshape(count, PB, tiles.shape[4])
    scale_rows = scales.reshape(count, scales.shape[3])
    slot_rows = slots.reshape(count, slots.shape[3])
    live_rows = live.reshape(count)
    total = features.astype(jnp.float32)
    factor = jnp.ones(times.shape, jnp.float32)
    value = features
    for term in range(1, TERMS + 1):
        image = apply_operator(value, tile_rows, scale_rows, slot_rows, live_rows)
        factor = factor * -times / jnp.float32(term)
        total = total + factor[:, None, None, None] * image
        value = image.astype(jnp.bfloat16)
    return total.astype(jnp.bfloat16)


def solution(mesh):
    return jax.shard_map(
        body,
        mesh=mesh,
        in_specs=(
            P(None, "gx", "gy", "gz"),
            P("gx", "gy", "gz", None, None),
            P("gx", "gy", "gz", None),
            P("gx", "gy", "gz", None),
            P("gx", "gy", "gz"),
            P(),
        ),
        out_specs=P(None, "gx", "gy", "gz"),
        check_vma=False,
    )
```

profile of v0, /device:TPU:0, one launch (start us, length us, event | category | flops | bytes accessed | tf_op | source)
XLA Modules:
  0.0 181.4 jit_solution(16395035376558209992)
XLA Ops:
  2.0 6.5 %all-gather = bf16[4,4,4096]{2,1,0:T(4,128)(2,1)S(1)} all-gather(bf16[1,4,4096]{2,1,0:T(4,128)(2,1)S(1)} %reshape.216), channel_id=1, replica_groups=mesh['gx'=2,'gy'=4,'gz'=4] {'gz'}, dimensions={0}, use_global_device_ids=true | all-gather | bytes 163840 | tf_op jit(solution)/shard_map/all_gather | solution.py:38
  8.5 3.8 %collective-permute-start = (bf16[1,1,16,4096]{3,2,1,0:T(8,128)(2,1)S(1)}, bf16[1,1,16,4096]{3,2,1,0:T(8,128)(2,1)S(1)}, u32[]{:S(2)}, u32[]{:S(2)}) collective-permute-start(bf16[1,1,16,4096]{3,2,1,0:T(8,128)(2,1)S(1)} %reshape.175), channel_id=1, source_target_pairs={{0,16},{1,17},{2,18},{3,19},{4,20},{5,21},{6,22},{7,23},{8,24},{9,... | collective-permute-start | bytes 393224 | tf_op jit(solution)/shard_map/ppermute | solution.py:18
  14.5 3.7 %reshape_reshape.5 = bf16[32,64,8,64]{3,2,1,0:T(8,128)(2,1)} reshape(bf16[1,1,32,64,512]{4,3,2,1,0:T(8,128)(2,1)S(1)} %copy-done.29) | data formatting | bytes 4194304 | tf_op jit(solution)/shard_map/reshape;reshape | solution.py:52
  18.1 23.5 %fusion.22 = (bf16[32,64,1,64]{3,2,1,0:T(2,128)(2,1)}, bf16[32,64,1,64]{3,2,1,0:T(2,128)(2,1)}, bf16[32,64,1,64]{3,2,1,0:T(2,128)(2,1)}, bf16[32,64,1,64]{3,2,1,...) fusion(bf16[32,64,8,64]{3,2,1,0:T(8,128)(2,1)} %reshape_reshape.5), kind=kLoop, calls=%fused_computation.116 | loop fusion | bytes 4194304 | tf_op jit(solution)/shard_map/slice | solution.py:62
  42.2 3.5 %collective-permute-start.2 = (bf16[3,1,16,4096]{3,2,1,0:T(8,128)(2,1)S(1)}, bf16[3,1,16,4096]{3,2,1,0:T(8,128)(2,1)S(1)}, u32[]{:S(2)}, u32[]{:S(2)}) collective-permute-start(bf16[3,1,16,4096]{3,2,1,0:T(8,128)(2,1)S(1)} %constant_dynamic-update-slice_fusion), channel_id=1, source_target_pairs={{0,4},{4,8},{8,12},{1,5},{5,9},{9,13},{2,6},{6,10},{10,14},{3,7},{... | collective-permute-start | bytes 1179656 | tf_op jit(solution)/shard_map/ppermute | solution.py:18
  48.2 6.1 %collective-permute-done.2 = bf16[3,1,16,4096]{3,2,1,0:T(8,128)(2,1)S(1)} collective-permute-done((bf16[3,1,16,4096]{3,2,1,0:T(8,128)(2,1)S(1)}, bf16[3,1,16,4096]{3,2,1,0:T(8,128)(2,1)S(1)}, u32[]{:S(2)}, u32[]{:S(2)}) %collective-permute-start.2) | collective-permute-done | bytes 393248 | tf_op jit(solution)/shard_map/ppermute | solution.py:18
  54.3 4.1 %collective-permute-done.3 = bf16[3,1,16,4096]{3,2,1,0:T(8,128)(2,1)S(1)} collective-permute-done((bf16[3,1,16,4096]{3,2,1,0:T(8,128)(2,1)S(1)}, bf16[3,1,16,4096]{3,2,1,0:T(8,128)(2,1)S(1)}, u32[]{:S(2)}, u32[]{:S(2)}) %collective-permute-start.3) | collective-permute-done | bytes 393248 | tf_op jit(solution)/shard_map/ppermute | solution.py:20
  60.6 2.3 %broadcast_select_fusion.2 = bf16[256,4096]{1,0:T(8,128)(2,1)} fusion(bf16[256,4096]{1,0:T(8,128)(2,1)S(1)} %gather_fusion, pred[256]{0:T(512)(128)(4,1)} %compare_and_fusion), kind=kLoop, calls=%fused_computation.5 | loop fusion | flops 1048576 | bytes 4194560 | tf_op jit(solution)/shard_map/jit(_take)/select_n | solution.py:49
  62.9 7.0 %reshape.177 = bf16[32,8,64,64]{3,2,1,0:T(8,128)(2,1)} reshape(bf16[256,4096]{1,0:T(8,128)(2,1)} %broadcast_select_fusion.2) | data formatting | bytes 4194304 | tf_op jit(solution)/shard_map/reshape | solution.py:49
  77.7 5.4 %all-gather.1 = bf16[4,4,4096]{2,1,0:T(4,128)(2,1)S(1)} all-gather(bf16[1,4,4096]{2,1,0:T(4,128)(2,1)S(1)} %reshape.218), channel_id=1, replica_groups=mesh['gx'=2,'gy'=4,'gz'=4] {'gz'}, dimensions={0}, use_global_device_ids=true | all-gather | bytes 163840 | tf_op jit(solution)/shard_map/all_gather | solution.py:38
  83.2 4.3 %collective-permute-start.4 = (bf16[1,1,16,4096]{3,2,1,0:T(8,128)(2,1)S(1)}, bf16[1,1,16,4096]{3,2,1,0:T(8,128)(2,1)S(1)}, u32[]{:S(2)}, u32[]{:S(2)}) collective-permute-start(bf16[1,1,16,4096]{3,2,1,0:T(8,128)(2,1)S(1)} %reshape.180), channel_id=1, source_target_pairs={{0,16},{1,17},{2,18},{3,19},{4,20},{5,21},{6,22},{7,23},{8,24},{9,... | collective-permute-start | bytes 393224 | tf_op jit(solution)/shard_map/ppermute | solution.py:18
  90.8 4.1 %collective-permute-done.5 = bf16[1,1,16,4096]{3,2,1,0:T(8,128)(2,1)S(1)} collective-permute-done((bf16[1,1,16,4096]{3,2,1,0:T(8,128)(2,1)S(1)}, bf16[1,1,16,4096]{3,2,1,0:T(8,128)(2,1)S(1)}, u32[]{:S(2)}, u32[]{:S(2)}) %collective-permute-start.5) | collective-permute-done | bytes 131104 | tf_op jit(solution)/shard_map/ppermute | solution.py:20
  94.9 3.5 %collective-permute-start.6 = (bf16[3,1,16,4096]{3,2,1,0:T(8,128)(2,1)S(1)}, bf16[3,1,16,4096]{3,2,1,0:T(8,128)(2,1)S(1)}, u32[]{:S(2)}, u32[]{:S(2)}) collective-permute-start(bf16[3,1,16,4096]{3,2,1,0:T(8,128)(2,1)S(1)} %constant_dynamic-update-slice_fusion.3), channel_id=1, source_target_pairs={{0,4},{4,8},{8,12},{1,5},{5,9},{9,13},{2,6},{6,10},{10,14},{3,7},{... | collective-permute-start | bytes 1179656 | tf_op jit(solution)/shard_map/ppermute | solution.py:18
  100.3 5.8 %collective-permute-done.6 = bf16[3,1,16,4096]{3,2,1,0:T(8,128)(2,1)S(1)} collective-permute-done((bf16[3,1,16,4096]{3,2,1,0:T(8,128)(2,1)S(1)}, bf16[3,1,16,4096]{3,2,1,0:T(8,128)(2,1)S(1)}, u32[]{:S(2)}, u32[]{:S(2)}) %collective-permute-start.6) | collective-permute-done | bytes 393248 | tf_op jit(solution)/shard_map/ppermute | solution.py:18
  106.1 4.1 %collective-permute-done.7 = bf16[3,1,16,4096]{3,2,1,0:T(8,128)(2,1)S(1)} collective-permute-done((bf16[3,1,16,4096]{3,2,1,0:T(8,128)(2,1)S(1)}, bf16[3,1,16,4096]{3,2,1,0:T(8,128)(2,1)S(1)}, u32[]{:S(2)}, u32[]{:S(2)}) %collective-permute-start.7) | collective-permute-done | bytes 393248 | tf_op jit(solution)/shard_map/ppermute | solution.py:20
  112.3 2.3 %broadcast_select_fusion.1 = bf16[256,4096]{1,0:T(8,128)(2,1)} fusion(bf16[256,4096]{1,0:T(8,128)(2,1)S(1)} %gather_fusion.1, pred[256]{0:T(512)(128)(4,1)} %compare_and_fusion), kind=kLoop, calls=%fused_computation.4 | loop fusion | flops 1048576 | bytes 4194560 | tf_op jit(solution)/shard_map/jit(_take)/select_n | solution.py:49
  114.6 7.0 %reshape.182 = bf16[32,8,64,64]{3,2,1,0:T(8,128)(2,1)} reshape(bf16[256,4096]{1,0:T(8,128)(2,1)} %broadcast_select_fusion.1) | data formatting | bytes 4194304 | tf_op jit(solution)/shard_map/reshape | solution.py:49
  129.3 5.4 %all-gather.2 = bf16[4,4,4096]{2,1,0:T(4,128)(2,1)S(1)} all-gather(bf16[1,4,4096]{2,1,0:T(4,128)(2,1)S(1)} %reshape.220), channel_id=1, replica_groups=mesh['gx'=2,'gy'=4,'gz'=4] {'gz'}, dimensions={0}, use_global_device_ids=true | all-gather | bytes 163840 | tf_op jit(solution)/shard_map/all_gather | solution.py:38
  137.6 2.1 %collective-permute-done.8 = bf16[1,1,16,4096]{3,2,1,0:T(8,128)(2,1)S(1)} collective-permute-done((bf16[1,1,16,4096]{3,2,1,0:T(8,128)(2,1)S(1)}, bf16[1,1,16,4096]{3,2,1,0:T(8,128)(2,1)S(1)}, u32[]{:S(2)}, u32[]{:S(2)}) %collective-permute-start.8) | collective-permute-done | bytes 131104 | tf_op jit(solution)/shard_map/ppermute | solution.py:18
  139.7 4.1 %collective-permute-done.9 = bf16[1,1,16,4096]{3,2,1,0:T(8,128)(2,1)S(1)} collective-permute-done((bf16[1,1,16,4096]{3,2,1,0:T(8,128)(2,1)S(1)}, bf16[1,1,16,4096]{3,2,1,0:T(8,128)(2,1)S(1)}, u32[]{:S(2)}, u32[]{:S(2)}) %collective-permute-start.9) | collective-permute-done | bytes 131104 | tf_op jit(solution)/shard_map/ppermute | solution.py:20
  143.8 4.2 %collective-permute-start.10 = (bf16[3,1,16,4096]{3,2,1,0:T(8,128)(2,1)S(1)}, bf16[3,1,16,4096]{3,2,1,0:T(8,128)(2,1)}, u32[]{:S(2)}, u32[]{:S(2)}) collective-permute-start(bf16[3,1,16,4096]{3,2,1,0:T(8,128)(2,1)S(1)} %constant_dynamic-update-slice_fusion.6), channel_id=1, source_target_pairs={{0,4},{4,8},{8,12},{1,5},{5,9},{9,13},{2,6},{6,10},{10,14},{3,7},{... | collective-permute-start | bytes 1179656 | tf_op jit(solution)/shard_map/ppermute | solution.py:18
  155.2 4.9 %collective-permute-done.11 = bf16[3,1,16,4096]{3,2,1,0:T(8,128)(2,1)} collective-permute-done((bf16[3,1,16,4096]{3,2,1,0:T(8,128)(2,1)S(1)}, bf16[3,1,16,4096]{3,2,1,0:T(8,128)(2,1)}, u32[]{:S(2)}, u32[]{:S(2)}) %collective-permute-start.11) | collective-permute-done | bytes 393248 | tf_op jit(solution)/shard_map/ppermute | solution.py:20
  163.3 2.3 %broadcast_select_fusion = bf16[256,4096]{1,0:T(8,128)(2,1)} fusion(bf16[256,4096]{1,0:T(8,128)(2,1)S(1)} %gather_fusion.2, pred[256]{0:T(512)(128)(4,1)} %compare_and_fusion), kind=kLoop, calls=%fused_computation.3 | loop fusion | flops 1048576 | bytes 4194560 | tf_op jit(solution)/shard_map/jit(_take)/select_n | solution.py:49
  165.6 7.0 %reshape.187 = bf16[32,8,64,64]{3,2,1,0:T(8,128)(2,1)} reshape(bf16[256,4096]{1,0:T(8,128)(2,1)} %broadcast_select_fusion) | data formatting | bytes 4194304 | tf_op jit(solution)/shard_map/reshape | solution.py:49
  (190 shorter events, 53.4 us)
Async XLA Ops:
  0.0 14.5 %copy-start.29 = (bf16[1,1,32,64,512]{4,3,2,1,0:T(8,128)(2,1)S(1)}, bf16[1,1,32,64,512]{4,3,2,1,0:T(8,128)(2,1)}, u32[]{:S(2)}) copy-start(bf16[1,1,32,64,512]{4,3,2,1,0:T(8,128)(2,1)} %param.9) | copy-start | bytes 6291460
  8.5 33.7 %collective-permute-start = (bf16[1,1,16,4096]{3,2,1,0:T(8,128)(2,1)S(1)}, bf16[1,1,16,4096]{3,2,1,0:T(8,128)(2,1)S(1)}, u32[]{:S(2)}, u32[]{:S(2)}) collective-permute-start(bf16[1,1,16,4096]{3,2,1,0:T(8,128)(2,1)S(1)} %reshape.175), channel_id=1, source_target_pairs={{0,16},{1,17},{2,18},{3,19},{4,20},{5,21},{6,22},{7,23},{8,24},{9,... | collective-permute-start | bytes 393224 | tf_op jit(solution)/shard_map/ppermute | solution.py:18
  12.3 29.9 %collective-permute-start.1 = (bf16[1,1,16,4096]{3,2,1,0:T(8,128)(2,1)S(1)}, bf16[1,1,16,4096]{3,2,1,0:T(8,128)(2,1)S(1)}, u32[]{:S(2)}, u32[]{:S(2)}) collective-permute-start(bf16[1,1,16,4096]{3,2,1,0:T(8,128)(2,1)S(1)} %reshape.175), channel_id=1, source_target_pairs={{16,0},{17,1},{18,2},{19,3},{20,4},{21,5},{22,6},{23,7},{24,8},{25... | collective-permute-start | bytes 393224 | tf_op jit(solution)/shard_map/ppermute | solution.py:20
  18.1 23.5 %copy-start.48 = (f32[1,1,32,8]{2,3,1,0:T(8,128)S(1)}, f32[1,1,32,8]{2,3,1,0:T(8,128)}, u32[]{:S(2)}) copy-start(f32[1,1,32,8]{2,3,1,0:T(8,128)} %param.10) | copy-start | bytes 3076
  18.1 23.5 %copy-start.52 = (s32[1,1,32]{2,1,0:T(1,128)S(1)}, s32[1,1,32]{2,1,0:T(1,128)}, u32[]{:S(2)}) copy-start(s32[1,1,32]{2,1,0:T(1,128)} %param.12) | copy-start | bytes 388
  42.2 12.1 %collective-permute-start.2 = (bf16[3,1,16,4096]{3,2,1,0:T(8,128)(2,1)S(1)}, bf16[3,1,16,4096]{3,2,1,0:T(8,128)(2,1)S(1)}, u32[]{:S(2)}, u32[]{:S(2)}) collective-permute-start(bf16[3,1,16,4096]{3,2,1,0:T(8,128)(2,1)S(1)} %constant_dynamic-update-slice_fusion), channel_id=1, source_target_pairs={{0,4},{4,8},{8,12},{1,5},{5,9},{9,13},{2,6},{6,10},{10,14},{3,7},{... | collective-permute-start | bytes 1179656 | tf_op jit(solution)/shard_map/ppermute | solution.py:18
  45.7 12.7 %collective-permute-start.3 = (bf16[3,1,16,4096]{3,2,1,0:T(8,128)(2,1)S(1)}, bf16[3,1,16,4096]{3,2,1,0:T(8,128)(2,1)S(1)}, u32[]{:S(2)}, u32[]{:S(2)}) collective-permute-start(bf16[3,1,16,4096]{3,2,1,0:T(8,128)(2,1)S(1)} %constant_dynamic-update-slice_fusion), channel_id=1, source_target_pairs={{4,0},{8,4},{12,8},{5,1},{9,5},{13,9},{6,2},{10,6},{14,10},{7,3},{... | collective-permute-start | bytes 1179656 | tf_op jit(solution)/shard_map/ppermute | solution.py:20
  62.8 7.1 %copy-start.3 = (bf16[32,64,1,64]{3,2,1,0:T(2,128)(2,1)S(1)}, bf16[32,64,1,64]{3,2,1,0:T(2,128)(2,1)}, u32[]{:S(2)}) copy-start(bf16[32,64,1,64]{3,2,1,0:T(2,128)(2,1)} %get-tuple-element.13) | copy-start | bytes 786436
  62.8 8.7 %copy-start.24 = (bf16[32,64,1,64]{3,2,1,0:T(2,128)(2,1)S(1)}, bf16[32,64,1,64]{3,2,1,0:T(2,128)(2,1)}, u32[]{:S(2)}) copy-start(bf16[32,64,1,64]{3,2,1,0:T(2,128)(2,1)} %get-tuple-element.12) | copy-start | bytes 786436
  62.9 8.7 %copy-start.42 = (f32[32]{0:T(128)S(1)}, f32[32]{0:T(128)}, u32[]{:S(2)}) copy-start(f32[32]{0:T(128)} %get-tuple-element.20) | copy-start | bytes 388
  83.2 7.5 %collective-permute-start.4 = (bf16[1,1,16,4096]{3,2,1,0:T(8,128)(2,1)S(1)}, bf16[1,1,16,4096]{3,2,1,0:T(8,128)(2,1)S(1)}, u32[]{:S(2)}, u32[]{:S(2)}) collective-permute-start(bf16[1,1,16,4096]{3,2,1,0:T(8,128)(2,1)S(1)} %reshape.180), channel_id=1, source_target_pairs={{0,16},{1,17},{2,18},{3,19},{4,20},{5,21},{6,22},{7,23},{8,24},{9,... | collective-permute-start | bytes 393224 | tf_op jit(solution)/shard_map/ppermute | solution.py:18
  87.5 7.4 %collective-permute-start.5 = (bf16[1,1,16,4096]{3,2,1,0:T(8,128)(2,1)S(1)}, bf16[1,1,16,4096]{3,2,1,0:T(8,128)(2,1)S(1)}, u32[]{:S(2)}, u32[]{:S(2)}) collective-permute-start(bf16[1,1,16,4096]{3,2,1,0:T(8,128)(2,1)S(1)} %reshape.180), channel_id=1, source_target_pairs={{16,0},{17,1},{18,2},{19,3},{20,4},{21,5},{22,6},{23,7},{24,8},{25... | collective-permute-start | bytes 393224 | tf_op jit(solution)/shard_map/ppermute | solution.py:20
  94.9 11.2 %collective-permute-start.6 = (bf16[3,1,16,4096]{3,2,1,0:T(8,128)(2,1)S(1)}, bf16[3,1,16,4096]{3,2,1,0:T(8,128)(2,1)S(1)}, u32[]{:S(2)}, u32[]{:S(2)}) collective-permute-start(bf16[3,1,16,4096]{3,2,1,0:T(8,128)(2,1)S(1)} %constant_dynamic-update-slice_fusion.3), channel_id=1, source_target_pairs={{0,4},{4,8},{8,12},{1,5},{5,9},{9,13},{2,6},{6,10},{10,14},{3,7},{... | collective-permute-start | bytes 1179656 | tf_op jit(solution)/shard_map/ppermute | solution.py:18
  98.4 11.9 %collective-permute-start.7 = (bf16[3,1,16,4096]{3,2,1,0:T(8,128)(2,1)S(1)}, bf16[3,1,16,4096]{3,2,1,0:T(8,128)(2,1)S(1)}, u32[]{:S(2)}, u32[]{:S(2)}) collective-permute-start(bf16[3,1,16,4096]{3,2,1,0:T(8,128)(2,1)S(1)} %constant_dynamic-update-slice_fusion.3), channel_id=1, source_target_pairs={{4,0},{8,4},{12,8},{5,1},{9,5},{13,9},{6,2},{10,6},{14,10},{7,3},{... | collective-permute-start | bytes 1179656 | tf_op jit(solution)/shard_map/ppermute | solution.py:20
  114.6 8.7 %copy-start.25 = (bf16[32,64,1,64]{3,2,1,0:T(2,128)(2,1)S(1)}, bf16[32,64,1,64]{3,2,1,0:T(2,128)(2,1)}, u32[]{:S(2)}) copy-start(bf16[32,64,1,64]{3,2,1,0:T(2,128)(2,1)} %get-tuple-element.12) | copy-start | bytes 786436
  114.6 8.7 %copy-start.43 = (f32[32]{0:T(128)S(1)}, f32[32]{0:T(128)}, u32[]{:S(2)}) copy-start(f32[32]{0:T(128)} %get-tuple-element.20) | copy-start | bytes 388
  128.0 21.5 %copy-start.53 = (f32[64]{0:T(128)S(1)}, f32[64]{0:T(128)}, u32[]{:S(2)}) copy-start(f32[64]{0:T(128)} %param.13) | copy-start | bytes 772
  128.0 22.1 %copy-start.27 = (f32[32,64,64]{2,1,0:T(8,128)S(1)}, f32[32,64,64]{2,1,0:T(8,128)}, u32[]{:S(2)}) copy-start(f32[32,64,64]{2,1,0:T(8,128)} %get-tuple-element.26) | copy-start | bytes 1572868
  134.8 4.8 %collective-permute-start.8 = (bf16[1,1,16,4096]{3,2,1,0:T(8,128)(2,1)S(1)}, bf16[1,1,16,4096]{3,2,1,0:T(8,128)(2,1)S(1)}, u32[]{:S(2)}, u32[]{:S(2)}) collective-permute-start(bf16[1,1,16,4096]{3,2,1,0:T(8,128)(2,1)S(1)} %reshape.185), channel_id=1, source_target_pairs={{0,16},{1,17},{2,18},{3,19},{4,20},{5,21},{6,22},{7,23},{8,24},{9,... | collective-permute-start | bytes 393224 | tf_op jit(solution)/shard_map/ppermute | solution.py:18
  136.3 7.5 %collective-permute-start.9 = (bf16[1,1,16,4096]{3,2,1,0:T(8,128)(2,1)S(1)}, bf16[1,1,16,4096]{3,2,1,0:T(8,128)(2,1)S(1)}, u32[]{:S(2)}, u32[]{:S(2)}) collective-permute-start(bf16[1,1,16,4096]{3,2,1,0:T(8,128)(2,1)S(1)} %reshape.185), channel_id=1, source_target_pairs={{16,0},{17,1},{18,2},{19,3},{20,4},{21,5},{22,6},{23,7},{24,8},{25... | collective-permute-start | bytes 393224 | tf_op jit(solution)/shard_map/ppermute | solution.py:20
  143.8 11.4 %collective-permute-start.10 = (bf16[3,1,16,4096]{3,2,1,0:T(8,128)(2,1)S(1)}, bf16[3,1,16,4096]{3,2,1,0:T(8,128)(2,1)}, u32[]{:S(2)}, u32[]{:S(2)}) collective-permute-start(bf16[3,1,16,4096]{3,2,1,0:T(8,128)(2,1)S(1)} %constant_dynamic-update-slice_fusion.6), channel_id=1, source_target_pairs={{0,4},{4,8},{8,12},{1,5},{5,9},{9,13},{2,6},{6,10},{10,14},{3,7},{... | collective-permute-start | bytes 1179656 | tf_op jit(solution)/shard_map/ppermute | solution.py:18
  148.0 12.1 %collective-permute-start.11 = (bf16[3,1,16,4096]{3,2,1,0:T(8,128)(2,1)S(1)}, bf16[3,1,16,4096]{3,2,1,0:T(8,128)(2,1)}, u32[]{:S(2)}, u32[]{:S(2)}) collective-permute-start(bf16[3,1,16,4096]{3,2,1,0:T(8,128)(2,1)S(1)} %constant_dynamic-update-slice_fusion.6), channel_id=1, source_target_pairs={{4,0},{8,4},{12,8},{5,1},{9,5},{13,9},{6,2},{10,6},{14,10},{7,3},{... | collective-permute-start | bytes 1179656 | tf_op jit(solution)/shard_map/ppermute | solution.py:20
  165.6 8.7 %copy-start.26 = (bf16[32,64,1,64]{3,2,1,0:T(2,128)(2,1)S(1)}, bf16[32,64,1,64]{3,2,1,0:T(2,128)(2,1)}, u32[]{:S(2)}) copy-start(bf16[32,64,1,64]{3,2,1,0:T(2,128)(2,1)} %get-tuple-element.12) | copy-start | bytes 786436
  165.6 8.7 %copy-start.44 = (f32[32]{0:T(128)S(1)}, f32[32]{0:T(128)}, u32[]{:S(2)}) copy-start(f32[32]{0:T(128)} %get-tuple-element.20) | copy-start | bytes 388
  (42 other events, 88.3 us)
where the time goes:
time: 182 us; the launch traced here: 181 us
  local copies, waits for them, and re-layouts  68.4 us (38%)
  waiting for transfers between devices  37.3 us (20%)
  starting transfers between devices  28.9 us (16%)
  matrix products  17.7 us (10%)
  blocking collectives  17.3 us (10%)
  other arithmetic  10.8 us (6%)
    slice x1, local copies, waits for them, and re-layouts, apply_operator(): tile_parts[:, :, slot]  23.5 us
    ppermute x6, waiting for transfers between devices, with_halo(): lax.ppermute(head, axis, [((i + 1) % count, i) for i in range(ends)])  21.4 us
    reshape x3, local copies, waits for them, and re-layouts, apply_operator(): jnp.take(source, slot_rows.reshape(-1), axis=0)  21.1 us
    ppermute x6, starting transfers between devices, with_halo(): lax.ppermute(tail, axis, [(i, (i + 1) % count) for i in range(ends)])  20.8 us
    dot_general x24, matrix products, apply_operator(): jnp.einsum('bfc,brc->bfr', picked[:, slot], tile_parts[:, :, slot], prefe...  17.7 us
    all_gather x3, blocking collectives, shared_blocks(): panel = lax.all_gather(rim_rows, 'gz', axis=0, tiled=True)  17.3 us
    ppermute x6, waiting for transfers between devices, with_halo(): lax.ppermute(tail, axis, [(i, (i + 1) % count) for i in range(ends)])  15.9 us
    ppermute x6, starting transfers between devices, with_halo(): lax.ppermute(head, axis, [((i + 1) % count, i) for i in range(ends)])  8.14 us
  transfers between devices with their start and end apart: 12, of which 9 were waited for; matrix products, arithmetic and copies ran while one was open for 20% of the time, Pallas kernels for 0%

commit v1 on v0

--- a/solution.py
+++ b/solution.py
@@ -35,7 +35,21 @@
 
 def shared_blocks(rim_rows):
     width = rim_rows.shape[1]
-    panel = lax.all_gather(rim_rows, "gz", axis=0, tiled=True)
+    ways, here, step = (lax.axis_size("gz"), lax.axis_index("gz"), rim_rows.shape[0])
+    dims = [n * ways if d == 0 else n for d, n in enumerate(rim_rows.shape)]
+    full = lax.dynamic_update_slice_in_dim(
+        jnp.zeros(dims, rim_rows.dtype), rim_rows, here * step, axis=0
+    )
+    going_up = going_down = rim_rows
+    for far in range(1, ways // 2 + 1):
+        going_up = lax.ppermute(going_up, "gz", [(d, (d + 1) % ways) for d in range(ways)])
+        full = lax.dynamic_update_slice_in_dim(full, going_up, (here - far) % ways * step, axis=0)
+        if 2 * far < ways:
+            going_down = lax.ppermute(going_down, "gz", [(d, (d - 1) % ways) for d in range(ways)])
+            full = lax.dynamic_update_slice_in_dim(
+                full, going_down, (here + far) % ways * step, axis=0
+            )
+    panel = full
     grid = with_halo(panel.reshape(1, 1, panel.shape[0], width), (("gx", 0), ("gy", 1)), 1)
     return grid.reshape(-1, width)
 

time: 182 us -> 189 us (1.038)
  blocking collectives: 17.3 us -> 0 us
  waiting for transfers between devices: 37.3 us -> 47.9 us
  local copies, waits for them, and re-layouts: 68.4 us -> 75.7 us
  starting transfers between devices: 28.9 us -> 33.7 us
    all_gather x3 -> x0, blocking collectives: 17.3 us -> none  [shared_blocks(): panel = lax.all_gather(rim_rows, 'gz', axis=0, tiled=True)]
    ppermute x0 -> x9, waiting for transfers between devices: none -> 12.3 us  [the longest x6 12.3 us: shared_blocks(): lax.ppermute(going_up, 'gz', [(d, (d + 1) % ways) for d in range(ways)])]
    unnamed x118 -> x111, local copies, waits for them, and re-layouts: 5 us -> 11.8 us
    ppermute x0 -> x9, starting transfers between devices: none -> 6.74 us  [the longest x3 5.45 us: shared_blocks(): lax.ppermute(going_down, 'gz', [(d, (d - 1) % ways) for d in range(ways)])]
    ppermute x6, waiting for transfers between devices: 15.9 us -> 10.5 us  [with_halo(): lax.ppermute(tail, axis, [(i, (i + 1) % count) for i in range(ends)])]
    ppermute x6, waiting for transfers between devices: 21.4 us -> 25.1 us  [with_halo(): lax.ppermute(head, axis, [((i + 1) % count, i) for i in range(ends)])]
    ppermute x6, starting transfers between devices: 20.8 us -> 18.8 us  [with_halo(): lax.ppermute(tail, axis, [(i, (i + 1) % count) for i in range(ends)])]
  transfers between devices with their start and end apart: 12 -> 21, of which waited for: 9 -> 16; matrix products, arithmetic and copies ran while one was open for 20% -> 19% of each run, Pallas kernels for 0% -> 0%
where the time goes in v1:
time: 189 us; the launch traced here: 188 us
  local copies, waits for them, and re-layouts  75.7 us (40%)
  waiting for transfers between devices  47.9 us (25%)
  starting transfers between devices  33.7 us (18%)
  matrix products  17.6 us (9%)
  other arithmetic  11.6 us (6%)
    ppermute x6, waiting for transfers between devices, with_halo(): lax.ppermute(head, axis, [((i + 1) % count, i) for i in range(ends)])  25.1 us
    slice x1, local copies, waits for them, and re-layouts, apply_operator(): tile_parts[:, :, slot]  23 us
    reshape x3, local copies, waits for them, and re-layouts, apply_operator(): jnp.take(source, slot_rows.reshape(-1), axis=0)  21.2 us
    ppermute x6, starting transfers between devices, with_halo(): lax.ppermute(tail, axis, [(i, (i + 1) % count) for i in range(ends)])  18.8 us
    dot_general x24, matrix products, apply_operator(): jnp.einsum('bfc,brc->bfr', picked[:, slot], tile_parts[:, :, slot], prefe...  17.6 us
    ppermute x6, waiting for transfers between devices, shared_blocks(): lax.ppermute(going_up, 'gz', [(d, (d + 1) % ways) for d in range(ways)])  12.3 us
    unnamed x111, local copies, waits for them, and re-layouts  11.8 us
    ppermute x6, waiting for transfers between devices, with_halo(): lax.ppermute(tail, axis, [(i, (i + 1) % count) for i in range(ends)])  10.5 us
  transfers between devices with their start and end apart: 21, of which 16 were waited for; matrix products, arithmetic and copies ran while one was open for 19% of the time, Pallas kernels for 0%

profile of v1, /device:TPU:0, one launch (start us, length us, event | category | flops | bytes accessed | tf_op | source)
XLA Modules:
  0.0 187.6 jit_solution(2849544399254748570)
XLA Ops:
  2.5 2.0 %collective-permute-start.1 = (bf16[4,4096]{1,0:T(4,128)(2,1)S(1)}, bf16[4,4096]{1,0:T(4,128)(2,1)S(1)}, u32[]{:S(2)}, u32[]{:S(2)}) collective-permute-start(bf16[4,4096]{1,0:T(4,128)(2,1)S(1)} %slice.172), channel_id=1, source_target_pairs={{0,3},{1,0},{2,1},{3,2},{4,7},{5,4},{6,5},{7,6},{8,11},{9,8},{10,9... | collective-permute-start | bytes 98312 | tf_op jit(solution)/shard_map/ppermute | solution.py:48
  4.6 3.6 %reshape_reshape.5 = bf16[32,64,8,64]{3,2,1,0:T(8,128)(2,1)} reshape(bf16[1,1,32,64,512]{4,3,2,1,0:T(8,128)(2,1)S(1)} %copy-done.29) | data formatting | bytes 4194304 | tf_op jit(solution)/shard_map/reshape;reshape | solution.py:66
  8.2 23.0 %fusion.22 = (bf16[32,64,1,64]{3,2,1,0:T(2,128)(2,1)}, bf16[32,64,1,64]{3,2,1,0:T(2,128)(2,1)}, bf16[32,64,1,64]{3,2,1,0:T(2,128)(2,1)}, bf16[32,64,1,64]{3,2,1,...) fusion(bf16[32,64,8,64]{3,2,1,0:T(8,128)(2,1)} %reshape_reshape.5), kind=kLoop, calls=%fused_computation.122 | loop fusion | bytes 4194304 | tf_op jit(solution)/shard_map/slice | solution.py:76
  32.3 2.6 %collective-permute-done.2 = bf16[4,4096]{1,0:T(4,128)(2,1)S(1)} collective-permute-done((bf16[4,4096]{1,0:T(4,128)(2,1)S(1)}, bf16[4,4096]{1,0:T(4,128)(2,1)S(1)}, u32[]{:S(2)}, u32[]{:S(2)}) %collective-permute-start.2) | collective-permute-done | bytes 32800 | tf_op jit(solution)/shard_map/ppermute | solution.py:45
  35.0 4.2 %collective-permute-start.3 = (bf16[1,1,16,4096]{3,2,1,0:T(8,128)(2,1)S(1)}, bf16[1,1,16,4096]{3,2,1,0:T(8,128)(2,1)S(1)}, u32[]{:S(2)}, u32[]{:S(2)}) collective-permute-start(bf16[1,1,16,4096]{3,2,1,0:T(8,128)(2,1)S(1)} %bitcast_dynamic-update-slice_fusion.6), channel_id=1, source_target_pairs={{0,16},{1,17},{2,18},{3,19},{4,20},{5,21},{6,22},{7,23},{8,24},{9,... | collective-permute-start | bytes 393224 | tf_op jit(solution)/shard_map/ppermute | solution.py:18
  41.7 4.4 %collective-permute-done.4 = bf16[1,1,16,4096]{3,2,1,0:T(8,128)(2,1)S(1)} collective-permute-done((bf16[1,1,16,4096]{3,2,1,0:T(8,128)(2,1)S(1)}, bf16[1,1,16,4096]{3,2,1,0:T(8,128)(2,1)S(1)}, u32[]{:S(2)}, u32[]{:S(2)}) %collective-permute-start.4) | collective-permute-done | bytes 131104 | tf_op jit(solution)/shard_map/ppermute | solution.py:20
  46.1 3.5 %collective-permute-start.5 = (bf16[3,1,16,4096]{3,2,1,0:T(8,128)(2,1)S(1)}, bf16[3,1,16,4096]{3,2,1,0:T(8,128)(2,1)S(1)}, u32[]{:S(2)}, u32[]{:S(2)}) collective-permute-start(bf16[3,1,16,4096]{3,2,1,0:T(8,128)(2,1)S(1)} %pad_maximum_fusion.6), channel_id=1, source_target_pairs={{0,4},{4,8},{8,12},{1,5},{5,9},{9,13},{2,6},{6,10},{10,14},{3,7},{... | collective-permute-start | bytes 1179656 | tf_op jit(solution)/shard_map/ppermute | solution.py:18
  52.1 3.9 %collective-permute-done.5 = bf16[3,1,16,4096]{3,2,1,0:T(8,128)(2,1)S(1)} collective-permute-done((bf16[3,1,16,4096]{3,2,1,0:T(8,128)(2,1)S(1)}, bf16[3,1,16,4096]{3,2,1,0:T(8,128)(2,1)S(1)}, u32[]{:S(2)}, u32[]{:S(2)}) %collective-permute-start.5) | collective-permute-done | bytes 393248 | tf_op jit(solution)/shard_map/ppermute | solution.py:18
  56.0 4.1 %collective-permute-done.6 = bf16[3,1,16,4096]{3,2,1,0:T(8,128)(2,1)S(1)} collective-permute-done((bf16[3,1,16,4096]{3,2,1,0:T(8,128)(2,1)S(1)}, bf16[3,1,16,4096]{3,2,1,0:T(8,128)(2,1)S(1)}, u32[]{:S(2)}, u32[]{:S(2)}) %collective-permute-start.6) | collective-permute-done | bytes 393248 | tf_op jit(solution)/shard_map/ppermute | solution.py:20
  62.3 2.3 %broadcast_select_fusion.2 = bf16[256,4096]{1,0:T(8,128)(2,1)} fusion(bf16[256,4096]{1,0:T(8,128)(2,1)S(1)} %gather_fusion, pred[256]{0:T(512)(128)(4,1)} %compare_and_fusion), kind=kLoop, calls=%fused_computation.5 | loop fusion | flops 1048576 | bytes 4194560 | tf_op jit(solution)/shard_map/jit(_take)/select_n | solution.py:63
  64.5 7.0 %reshape.228 = bf16[32,8,64,64]{3,2,1,0:T(8,128)(2,1)} reshape(bf16[256,4096]{1,0:T(8,128)(2,1)} %broadcast_select_fusion.2) | data formatting | bytes 4194304 | tf_op jit(solution)/shard_map/reshape | solution.py:63
  84.5 3.3 %collective-permute-done.9 = bf16[4,4096]{1,0:T(4,128)(2,1)S(1)} collective-permute-done((bf16[4,4096]{1,0:T(4,128)(2,1)S(1)}, bf16[4,4096]{1,0:T(4,128)(2,1)S(1)}, u32[]{:S(2)}, u32[]{:S(2)}) %collective-permute-start.9) | collective-permute-done | bytes 32800 | tf_op jit(solution)/shard_map/ppermute | solution.py:45
  92.1 4.4 %collective-permute-done.11 = bf16[1,1,16,4096]{3,2,1,0:T(8,128)(2,1)S(1)} collective-permute-done((bf16[1,1,16,4096]{3,2,1,0:T(8,128)(2,1)S(1)}, bf16[1,1,16,4096]{3,2,1,0:T(8,128)(2,1)S(1)}, u32[]{:S(2)}, u32[]{:S(2)}) %collective-permute-start.11) | collective-permute-done | bytes 131104 | tf_op jit(solution)/shard_map/ppermute | solution.py:20
  96.5 3.5 %collective-permute-start.12 = (bf16[3,1,16,4096]{3,2,1,0:T(8,128)(2,1)S(1)}, bf16[3,1,16,4096]{3,2,1,0:T(8,128)(2,1)S(1)}, u32[]{:S(2)}, u32[]{:S(2)}) collective-permute-start(bf16[3,1,16,4096]{3,2,1,0:T(8,128)(2,1)S(1)} %pad_maximum_fusion.7), channel_id=1, source_target_pairs={{0,4},{4,8},{8,12},{1,5},{5,9},{9,13},{2,6},{6,10},{10,14},{3,7},{... | collective-permute-start | bytes 1179656 | tf_op jit(solution)/shard_map/ppermute | solution.py:18
  101.9 3.5 %collective-permute-done.12 = bf16[3,1,16,4096]{3,2,1,0:T(8,128)(2,1)S(1)} collective-permute-done((bf16[3,1,16,4096]{3,2,1,0:T(8,128)(2,1)S(1)}, bf16[3,1,16,4096]{3,2,1,0:T(8,128)(2,1)S(1)}, u32[]{:S(2)}, u32[]{:S(2)}) %collective-permute-start.12) | collective-permute-done | bytes 393248 | tf_op jit(solution)/shard_map/ppermute | solution.py:18
  105.4 4.3 %collective-permute-done.13 = bf16[3,1,16,4096]{3,2,1,0:T(8,128)(2,1)S(1)} collective-permute-done((bf16[3,1,16,4096]{3,2,1,0:T(8,128)(2,1)S(1)}, bf16[3,1,16,4096]{3,2,1,0:T(8,128)(2,1)S(1)}, u32[]{:S(2)}, u32[]{:S(2)}) %collective-permute-start.13) | collective-permute-done | bytes 393248 | tf_op jit(solution)/shard_map/ppermute | solution.py:20
  111.8 2.3 %broadcast_select_fusion.1 = bf16[256,4096]{1,0:T(8,128)(2,1)} fusion(bf16[256,4096]{1,0:T(8,128)(2,1)S(1)} %gather_fusion.1, pred[256]{0:T(512)(128)(4,1)} %compare_and_fusion), kind=kLoop, calls=%fused_computation.4 | loop fusion | flops 1048576 | bytes 4194560 | tf_op jit(solution)/shard_map/jit(_take)/select_n | solution.py:63
  114.0 7.1 %reshape.236 = bf16[32,8,64,64]{3,2,1,0:T(8,128)(2,1)} reshape(bf16[256,4096]{1,0:T(8,128)(2,1)} %broadcast_select_fusion.1) | data formatting | bytes 4194304 | tf_op jit(solution)/shard_map/reshape | solution.py:63
  135.4 3.3 %collective-permute-done.16 = bf16[4,4096]{1,0:T(4,128)(2,1)S(1)} collective-permute-done((bf16[4,4096]{1,0:T(4,128)(2,1)S(1)}, bf16[4,4096]{1,0:T(4,128)(2,1)S(1)}, u32[]{:S(2)}, u32[]{:S(2)}) %collective-permute-start.16) | collective-permute-done | bytes 32800 | tf_op jit(solution)/shard_map/ppermute | solution.py:45
  142.9 4.4 %collective-permute-done.18 = bf16[1,1,16,4096]{3,2,1,0:T(8,128)(2,1)S(1)} collective-permute-done((bf16[1,1,16,4096]{3,2,1,0:T(8,128)(2,1)S(1)}, bf16[1,1,16,4096]{3,2,1,0:T(8,128)(2,1)S(1)}, u32[]{:S(2)}, u32[]{:S(2)}) %collective-permute-start.18) | collective-permute-done | bytes 131104 | tf_op jit(solution)/shard_map/ppermute | solution.py:20
  148.0 4.2 %collective-permute-start.19 = (bf16[3,1,16,4096]{3,2,1,0:T(8,128)(2,1)}, bf16[3,1,16,4096]{3,2,1,0:T(8,128)(2,1)}, u32[]{:S(2)}, u32[]{:S(2)}) collective-permute-start(bf16[3,1,16,4096]{3,2,1,0:T(8,128)(2,1)} %pad_maximum_fusion.8), channel_id=1, source_target_pairs={{0,4},{4,8},{8,12},{1,5},{5,9},{9,13},{2,6},{6,10},{10,14},{3,7},{... | collective-permute-start | bytes 1179656 | tf_op jit(solution)/shard_map/ppermute | solution.py:18
  159.4 3.6 %collective-permute-done.20 = bf16[3,1,16,4096]{3,2,1,0:T(8,128)(2,1)} collective-permute-done((bf16[3,1,16,4096]{3,2,1,0:T(8,128)(2,1)}, bf16[3,1,16,4096]{3,2,1,0:T(8,128)(2,1)}, u32[]{:S(2)}, u32[]{:S(2)}) %collective-permute-start.20) | collective-permute-done | bytes 393248 | tf_op jit(solution)/shard_map/ppermute | solution.py:20
  166.3 2.3 %broadcast_select_fusion = bf16[256,4096]{1,0:T(8,128)(2,1)} fusion(bf16[256,4096]{1,0:T(8,128)(2,1)S(1)} %gather_fusion.2, pred[256]{0:T(512)(128)(4,1)} %compare_and_fusion), kind=kLoop, calls=%fused_computation.3 | loop fusion | flops 1048576 | bytes 4194560 | tf_op jit(solution)/shard_map/jit(_take)/select_n | solution.py:63
  168.6 7.1 %reshape.244 = bf16[32,8,64,64]{3,2,1,0:T(8,128)(2,1)} reshape(bf16[256,4096]{1,0:T(8,128)(2,1)} %broadcast_select_fusion) | data formatting | bytes 4194304 | tf_op jit(solution)/shard_map/reshape | solution.py:63
  (216 shorter events, 72.9 us)
Async XLA Ops:
  2.0 29.6 %collective-permute-start = (bf16[4,4096]{1,0:T(4,128)(2,1)S(1)}, bf16[4,4096]{1,0:T(4,128)(2,1)S(1)}, u32[]{:S(2)}, u32[]{:S(2)}) collective-permute-start(bf16[4,4096]{1,0:T(4,128)(2,1)S(1)} %slice.172), channel_id=1, source_target_pairs={{0,1},{1,2},{2,3},{3,0},{4,5},{5,6},{6,7},{7,4},{8,9},{9,10},{10,1... | collective-permute-start | bytes 98312 | tf_op jit(solution)/shard_map/ppermute | solution.py:45
  2.5 29.8 %collective-permute-start.1 = (bf16[4,4096]{1,0:T(4,128)(2,1)S(1)}, bf16[4,4096]{1,0:T(4,128)(2,1)S(1)}, u32[]{:S(2)}, u32[]{:S(2)}) collective-permute-start(bf16[4,4096]{1,0:T(4,128)(2,1)S(1)} %slice.172), channel_id=1, source_target_pairs={{0,3},{1,0},{2,1},{3,2},{4,7},{5,4},{6,5},{7,6},{8,11},{9,8},{10,9... | collective-permute-start | bytes 98312 | tf_op jit(solution)/shard_map/ppermute | solution.py:48
  8.2 23.2 %copy-start.48 = (s32[1,1,32,8]{2,3,1,0:T(8,128)S(1)}, s32[1,1,32,8]{2,3,1,0:T(8,128)}, u32[]{:S(2)}) copy-start(s32[1,1,32,8]{2,3,1,0:T(8,128)} %param.11) | copy-start | bytes 3076
  31.6 3.4 %collective-permute-start.2 = (bf16[4,4096]{1,0:T(4,128)(2,1)S(1)}, bf16[4,4096]{1,0:T(4,128)(2,1)S(1)}, u32[]{:S(2)}, u32[]{:S(2)}) collective-permute-start(bf16[4,4096]{1,0:T(4,128)(2,1)S(1)} %collective-permute-done), channel_id=1, source_target_pairs={{0,1},{1,2},{2,3},{3,0},{4,5},{5,6},{6,7},{7,4},{8,9},{9,10},{10,1... | collective-permute-start | bytes 98312 | tf_op jit(solution)/shard_map/ppermute | solution.py:45
  35.0 6.7 %collective-permute-start.3 = (bf16[1,1,16,4096]{3,2,1,0:T(8,128)(2,1)S(1)}, bf16[1,1,16,4096]{3,2,1,0:T(8,128)(2,1)S(1)}, u32[]{:S(2)}, u32[]{:S(2)}) collective-permute-start(bf16[1,1,16,4096]{3,2,1,0:T(8,128)(2,1)S(1)} %bitcast_dynamic-update-slice_fusion.6), channel_id=1, source_target_pairs={{0,16},{1,17},{2,18},{3,19},{4,20},{5,21},{6,22},{7,23},{8,24},{9,... | collective-permute-start | bytes 393224 | tf_op jit(solution)/shard_map/ppermute | solution.py:18
  39.2 6.9 %collective-permute-start.4 = (bf16[1,1,16,4096]{3,2,1,0:T(8,128)(2,1)S(1)}, bf16[1,1,16,4096]{3,2,1,0:T(8,128)(2,1)S(1)}, u32[]{:S(2)}, u32[]{:S(2)}) collective-permute-start(bf16[1,1,16,4096]{3,2,1,0:T(8,128)(2,1)S(1)} %bitcast_dynamic-update-slice_fusion.6), channel_id=1, source_target_pairs={{16,0},{17,1},{18,2},{19,3},{20,4},{21,5},{22,6},{23,7},{24,8},{25... | collective-permute-start | bytes 393224 | tf_op jit(solution)/shard_map/ppermute | solution.py:20
  46.1 9.9 %collective-permute-start.5 = (bf16[3,1,16,4096]{3,2,1,0:T(8,128)(2,1)S(1)}, bf16[3,1,16,4096]{3,2,1,0:T(8,128)(2,1)S(1)}, u32[]{:S(2)}, u32[]{:S(2)}) collective-permute-start(bf16[3,1,16,4096]{3,2,1,0:T(8,128)(2,1)S(1)} %pad_maximum_fusion.6), channel_id=1, source_target_pairs={{0,4},{4,8},{8,12},{1,5},{5,9},{9,13},{2,6},{6,10},{10,14},{3,7},{... | collective-permute-start | bytes 1179656 | tf_op jit(solution)/shard_map/ppermute | solution.py:18
  49.6 10.5 %collective-permute-start.6 = (bf16[3,1,16,4096]{3,2,1,0:T(8,128)(2,1)S(1)}, bf16[3,1,16,4096]{3,2,1,0:T(8,128)(2,1)S(1)}, u32[]{:S(2)}, u32[]{:S(2)}) collective-permute-start(bf16[3,1,16,4096]{3,2,1,0:T(8,128)(2,1)S(1)} %pad_maximum_fusion.6), channel_id=1, source_target_pairs={{4,0},{8,4},{12,8},{5,1},{9,5},{13,9},{6,2},{10,6},{14,10},{7,3},{... | collective-permute-start | bytes 1179656 | tf_op jit(solution)/shard_map/ppermute | solution.py:20
  81.0 3.4 %collective-permute-start.7 = (bf16[4,4096]{1,0:T(4,128)(2,1)S(1)}, bf16[4,4096]{1,0:T(4,128)(2,1)S(1)}, u32[]{:S(2)}, u32[]{:S(2)}) collective-permute-start(bf16[4,4096]{1,0:T(4,128)(2,1)S(1)} %slice.197), channel_id=1, source_target_pairs={{0,1},{1,2},{2,3},{3,0},{4,5},{5,6},{6,7},{7,4},{8,9},{9,10},{10,1... | collective-permute-start | bytes 98312 | tf_op jit(solution)/shard_map/ppermute | solution.py:45
  81.1 3.4 %collective-permute-start.8 = (bf16[4,4096]{1,0:T(4,128)(2,1)S(1)}, bf16[4,4096]{1,0:T(4,128)(2,1)S(1)}, u32[]{:S(2)}, u32[]{:S(2)}) collective-permute-start(bf16[4,4096]{1,0:T(4,128)(2,1)S(1)} %slice.197), channel_id=1, source_target_pairs={{0,3},{1,0},{2,1},{3,2},{4,7},{5,4},{6,5},{7,6},{8,11},{9,8},{10,9... | collective-permute-start | bytes 98312 | tf_op jit(solution)/shard_map/ppermute | solution.py:48
  84.4 3.3 %collective-permute-start.9 = (bf16[4,4096]{1,0:T(4,128)(2,1)S(1)}, bf16[4,4096]{1,0:T(4,128)(2,1)S(1)}, u32[]{:S(2)}, u32[]{:S(2)}) collective-permute-start(bf16[4,4096]{1,0:T(4,128)(2,1)S(1)} %collective-permute-done.7), channel_id=1, source_target_pairs={{0,1},{1,2},{2,3},{3,0},{4,5},{5,6},{6,7},{7,4},{8,9},{9,10},{10,1... | collective-permute-start | bytes 98312 | tf_op jit(solution)/shard_map/ppermute | solution.py:45
  87.8 4.3 %collective-permute-start.10 = (bf16[1,1,16,4096]{3,2,1,0:T(8,128)(2,1)S(1)}, bf16[1,1,16,4096]{3,2,1,0:T(8,128)(2,1)S(1)}, u32[]{:S(2)}, u32[]{:S(2)}) collective-permute-start(bf16[1,1,16,4096]{3,2,1,0:T(8,128)(2,1)S(1)} %bitcast_dynamic-update-slice_fusion.3), channel_id=1, source_target_pairs={{0,16},{1,17},{2,18},{3,19},{4,20},{5,21},{6,22},{7,23},{8,24},{9,... | collective-permute-start | bytes 393224 | tf_op jit(solution)/shard_map/ppermute | solution.py:18
  89.6 6.9 %collective-permute-start.11 = (bf16[1,1,16,4096]{3,2,1,0:T(8,128)(2,1)S(1)}, bf16[1,1,16,4096]{3,2,1,0:T(8,128)(2,1)S(1)}, u32[]{:S(2)}, u32[]{:S(2)}) collective-permute-start(bf16[1,1,16,4096]{3,2,1,0:T(8,128)(2,1)S(1)} %bitcast_dynamic-update-slice_fusion.3), channel_id=1, source_target_pairs={{16,0},{17,1},{18,2},{19,3},{20,4},{21,5},{22,6},{23,7},{24,8},{25... | collective-permute-start | bytes 393224 | tf_op jit(solution)/shard_map/ppermute | solution.py:20
  96.5 8.9 %collective-permute-start.12 = (bf16[3,1,16,4096]{3,2,1,0:T(8,128)(2,1)S(1)}, bf16[3,1,16,4096]{3,2,1,0:T(8,128)(2,1)S(1)}, u32[]{:S(2)}, u32[]{:S(2)}) collective-permute-start(bf16[3,1,16,4096]{3,2,1,0:T(8,128)(2,1)S(1)} %pad_maximum_fusion.7), channel_id=1, source_target_pairs={{0,4},{4,8},{8,12},{1,5},{5,9},{9,13},{2,6},{6,10},{10,14},{3,7},{... | collective-permute-start | bytes 1179656 | tf_op jit(solution)/shard_map/ppermute | solution.py:18
  100.0 9.7 %collective-permute-start.13 = (bf16[3,1,16,4096]{3,2,1,0:T(8,128)(2,1)S(1)}, bf16[3,1,16,4096]{3,2,1,0:T(8,128)(2,1)S(1)}, u32[]{:S(2)}, u32[]{:S(2)}) collective-permute-start(bf16[3,1,16,4096]{3,2,1,0:T(8,128)(2,1)S(1)} %pad_maximum_fusion.7), channel_id=1, source_target_pairs={{4,0},{8,4},{12,8},{5,1},{9,5},{13,9},{6,2},{10,6},{14,10},{7,3},{... | collective-permute-start | bytes 1179656 | tf_op jit(solution)/shard_map/ppermute | solution.py:20
  130.5 23.3 %copy-start.54 = (f32[64]{0:T(128)S(1)}, f32[64]{0:T(128)}, u32[]{:S(2)}) copy-start(f32[64]{0:T(128)} %param.13) | copy-start | bytes 772
  130.5 23.9 %copy-start.27 = (f32[32,64,64]{2,1,0:T(8,128)S(1)}, f32[32,64,64]{2,1,0:T(8,128)}, u32[]{:S(2)}) copy-start(f32[32,64,64]{2,1,0:T(8,128)} %get-tuple-element.26) | copy-start | bytes 1572868
  131.9 3.4 %collective-permute-start.14 = (bf16[4,4096]{1,0:T(4,128)(2,1)S(1)}, bf16[4,4096]{1,0:T(4,128)(2,1)S(1)}, u32[]{:S(2)}, u32[]{:S(2)}) collective-permute-start(bf16[4,4096]{1,0:T(4,128)(2,1)S(1)} %slice.207), channel_id=1, source_target_pairs={{0,1},{1,2},{2,3},{3,0},{4,5},{5,6},{6,7},{7,4},{8,9},{9,10},{10,1... | collective-permute-start | bytes 98312 | tf_op jit(solution)/shard_map/ppermute | solution.py:45
  132.0 3.4 %collective-permute-start.15 = (bf16[4,4096]{1,0:T(4,128)(2,1)S(1)}, bf16[4,4096]{1,0:T(4,128)(2,1)S(1)}, u32[]{:S(2)}, u32[]{:S(2)}) collective-permute-start(bf16[4,4096]{1,0:T(4,128)(2,1)S(1)} %slice.207), channel_id=1, source_target_pairs={{0,3},{1,0},{2,1},{3,2},{4,7},{5,4},{6,5},{7,6},{8,11},{9,8},{10,9... | collective-permute-start | bytes 98312 | tf_op jit(solution)/shard_map/ppermute | solution.py:48
  135.3 3.3 %collective-permute-start.16 = (bf16[4,4096]{1,0:T(4,128)(2,1)S(1)}, bf16[4,4096]{1,0:T(4,128)(2,1)S(1)}, u32[]{:S(2)}, u32[]{:S(2)}) collective-permute-start(bf16[4,4096]{1,0:T(4,128)(2,1)S(1)} %collective-permute-done.14), channel_id=1, source_target_pairs={{0,1},{1,2},{2,3},{3,0},{4,5},{5,6},{6,7},{7,4},{8,9},{9,10},{10,1... | collective-permute-start | bytes 98312 | tf_op jit(solution)/shard_map/ppermute | solution.py:45
  138.7 4.2 %collective-permute-start.17 = (bf16[1,1,16,4096]{3,2,1,0:T(8,128)(2,1)S(1)}, bf16[1,1,16,4096]{3,2,1,0:T(8,128)(2,1)S(1)}, u32[]{:S(2)}, u32[]{:S(2)}) collective-permute-start(bf16[1,1,16,4096]{3,2,1,0:T(8,128)(2,1)S(1)} %bitcast_dynamic-update-slice_fusion), channel_id=1, source_target_pairs={{0,16},{1,17},{2,18},{3,19},{4,20},{5,21},{6,22},{7,23},{8,24},{9,... | collective-permute-start | bytes 393224 | tf_op jit(solution)/shard_map/ppermute | solution.py:18
  140.4 6.9 %collective-permute-start.18 = (bf16[1,1,16,4096]{3,2,1,0:T(8,128)(2,1)S(1)}, bf16[1,1,16,4096]{3,2,1,0:T(8,128)(2,1)S(1)}, u32[]{:S(2)}, u32[]{:S(2)}) collective-permute-start(bf16[1,1,16,4096]{3,2,1,0:T(8,128)(2,1)S(1)} %bitcast_dynamic-update-slice_fusion), channel_id=1, source_target_pairs={{16,0},{17,1},{18,2},{19,3},{20,4},{21,5},{22,6},{23,7},{24,8},{25... | collective-permute-start | bytes 393224 | tf_op jit(solution)/shard_map/ppermute | solution.py:20
  148.0 11.4 %collective-permute-start.19 = (bf16[3,1,16,4096]{3,2,1,0:T(8,128)(2,1)}, bf16[3,1,16,4096]{3,2,1,0:T(8,128)(2,1)}, u32[]{:S(2)}, u32[]{:S(2)}) collective-permute-start(bf16[3,1,16,4096]{3,2,1,0:T(8,128)(2,1)} %pad_maximum_fusion.8), channel_id=1, source_target_pairs={{0,4},{4,8},{8,12},{1,5},{5,9},{9,13},{2,6},{6,10},{10,14},{3,7},{... | collective-permute-start | bytes 1179656 | tf_op jit(solution)/shard_map/ppermute | solution.py:18
  152.2 10.8 %collective-permute-start.20 = (bf16[3,1,16,4096]{3,2,1,0:T(8,128)(2,1)}, bf16[3,1,16,4096]{3,2,1,0:T(8,128)(2,1)}, u32[]{:S(2)}, u32[]{:S(2)}) collective-permute-start(bf16[3,1,16,4096]{3,2,1,0:T(8,128)(2,1)} %pad_maximum_fusion.8), channel_id=1, source_target_pairs={{4,0},{8,4},{12,8},{5,1},{9,5},{13,9},{6,2},{10,6},{14,10},{7,3},{... | collective-permute-start | bytes 1179656 | tf_op jit(solution)/shard_map/ppermute | solution.py:20
  (52 other events, 173.9 us)
